TPU v7x, 32 devices: a whole 2x2x4 slice. The times are simulated.
32 devices in a mesh: lon: 8 (over z, x), lat: 4 (over y, core).
Axes of the slice: x: 2, y: 2, z: 4, core: 2. Of those that a mesh axis runs over, the one named last changes fastest.
Arguments:
- fields: bfloat16 [128, 256, 256], P('lat', 'lon'), may hold values from -6 to 6
- cotangent: bfloat16 [128, 256, 256], P('lat', 'lon'), may hold values from -6 to 6
- dw_kernel: bfloat16 [7, 7, 256], replicated, may hold values from -0.875 to 0.875
- dw_bias: bfloat16 [256], replicated, may hold values from -3 to 3
- norm_gain: bfloat16 [256], replicated, may hold values from 0.099609375 to 1.8984375
- layer_norm_offset: bfloat16 [256], replicated, may hold values from -3 to 3
- w_expand: bfloat16 [256, 1024], replicated, may hold values from -0.375 to 0.375
- b_expand: bfloat16 [1024], replicated, may hold values from -3 to 3
- w_project: bfloat16 [1024, 256], replicated, may hold values from -0.1875 to 0.1875
- b_project: bfloat16 [256], replicated, may hold values from -3 to 3
Outputs:
- block_out: bfloat16 [128, 256, 256], P('lat', 'lon')
- grad_fields: bfloat16 [128, 256, 256], P('lat', 'lon')
- grad_kernel: float32 [7, 7, 256], replicated
- grad_dw_bias: float32 [256], replicated
- grad_gain: float32 [256], replicated
- grad_shift: float32 [256], replicated
- grad_expand: float32 [256, 1024], replicated
- grad_b_expand: float32 [1024], replicated
- grad_project: float32 [1024, 256], replicated
- grad_b_project: float32 [256], replicated
All inputs are finite; a program needn't handle non-finite values.
Results may differ from a plain program's by a relative error of at most 0.0075.
Values may be sent and summed in bfloat16 or wider, within the bound.
No kernel may reach another device: no remote copies, remote signals or barrier semaphores. Data moves between devices by JAX's collectives and lax.ppermute only.
A program may use at most 64 MiB of HBM per device.

v0:
```python
import math
import jax
import jax.numpy as jnp
from jax import lax
from jax.sharding import PartitionSpec as P

EPS = 1e-06


def extended(array, sides, width, wrap):
    for axis, dim in sides:
        size, length = (lax.axis_size(axis), array.shape[dim])
        up = [(i, (i + 1) % size) for i in range(size if wrap else size - 1)]
        down = [(j, i) for i, j in up]
        last = lax.slice_in_dim(array, length - width, length, axis=dim)
        first = lax.slice_in_dim(array, 0, width, axis=dim)
        before = lax.ppermute(last, axis, up)
        after = lax.ppermute(first, axis, down)
        array = jnp.concatenate([before, array, after], axis=dim)
    return array


def from_behind(value, axis, steps):
    count = lax.axis_size(axis)
    pairs = [(source, (source + steps) % count) for source in range(count)]
    return lax.ppermute(value, axis, pairs)


def gelu_parts(values):
    normal_cdf = 0.5 * (1.0 + jax.scipy.special.erf(values * (1.0 / math.sqrt(2.0))))
    density = jnp.exp(-0.5 * values * values) * (1.0 / math.sqrt(2.0 * math.pi))
    return (values * normal_cdf, normal_cdf + values * density)


def contract_rows(left, right):
    return lax.dot_general(
        left, right, (((0,), (0,)), ((), ())), preferred_element_type=jnp.float32
    )


def sphere_pad(field):
    lat_index = lax.axis_index("lat")
    north = lat_index == 0
    south = lat_index == lax.axis_size("lat") - 1
    wide = extended(field, (("lon", 1),), 3, True)
    outgoing = jnp.where(north, wide[2::-1], wide[:-4:-1])
    partner = from_behind(outgoing, "lon", lax.axis_size("lon") // 2)
    tall = extended(wide, (("lat", 0),), 3, False)
    top_rows = jnp.where(north, partner, tall[:3])
    bottom_rows = jnp.where(south, partner, tall[-3:])
    return (jnp.concatenate([top_rows, tall[3:-3], bottom_rows], axis=0), north, south)


def local(
    fields,
    cotangent,
    dw_kernel,
    dw_bias,
    norm_gain,
    layer_norm_offset,
    w_expand,
    b_expand,
    w_project,
    b_project,
):
    rows = fields.shape[0]
    cols = fields.shape[1]
    chans = fields.shape[2]
    scale_factor = 1.0 / math.sqrt(rows * cols * lax.axis_size("lat") * lax.axis_size("lon"))
    weights = dw_kernel.astype(jnp.float32)
    norm_scale_factor = norm_gain.astype(jnp.float32)
    padded, north, south = sphere_pad(fields)
    conv = jnp.zeros((rows, cols, chans), jnp.float32)
    for row_off in range(7):
        for col_off in range(7):
            conv = conv + weights[row_off, col_off] * padded[
                row_off : row_off + rows, col_off : col_off + cols
            ].astype(jnp.float32)
    conv = conv.reshape(-1, chans) + dw_bias.astype(jnp.float32)
    mean_removed = conv - jnp.mean(conv, axis=-1, keepdims=True)
    inverse_deviation = lax.rsqrt(
        jnp.mean(mean_removed * mean_removed, axis=-1, keepdims=True) + EPS
    )
    standardized_input = mean_removed * inverse_deviation
    normalized_input = (
        standardized_input * norm_scale_factor + layer_norm_offset.astype(jnp.float32)
    ).astype(jnp.bfloat16)
    pre = jnp.dot(normalized_input, w_expand, preferred_element_type=jnp.float32) + b_expand.astype(
        jnp.float32
    )
    active, slope = gelu_parts(pre)
    hidden = active.astype(jnp.bfloat16)
    branch = jnp.dot(hidden, w_project, preferred_element_type=jnp.float32) + b_project.astype(
        jnp.float32
    )
    flat_fields = fields.reshape(-1, chans)
    block_out = (
        (flat_fields.astype(jnp.float32) + branch).astype(jnp.bfloat16).reshape(rows, cols, chans)
    )
    flat_cot = cotangent.reshape(-1, chans)
    grad_proj = contract_rows(hidden, flat_cot) * scale_factor
    grad_bproj = jnp.sum(flat_cot.astype(jnp.float32), axis=0) * scale_factor
    d_hidden = jnp.dot(flat_cot, w_project.T, preferred_element_type=jnp.float32)
    d_pre = (d_hidden * slope).astype(jnp.bfloat16)
    grad_exp = contract_rows(normalized_input, d_pre) * scale_factor
    grad_bexp = jnp.sum(d_pre.astype(jnp.float32), axis=0) * scale_factor
    normalized_gradient = jnp.dot(d_pre, w_expand.T, preferred_element_type=jnp.float32)
    gain_gradient = jnp.sum(normalized_gradient * standardized_input, axis=0) * scale_factor
    grad_sh = jnp.sum(normalized_gradient, axis=0) * scale_factor
    scaled_output = normalized_gradient * norm_scale_factor
    conv_gradient = inverse_deviation * (
        scaled_output
        - jnp.mean(scaled_output, axis=-1, keepdims=True)
        - standardized_input * jnp.mean(scaled_output * standardized_input, axis=-1, keepdims=True)
    )
    conv_gradient = conv_gradient.astype(jnp.bfloat16).reshape(rows, cols, chans)
    grad_dwb = jnp.sum(conv_gradient.astype(jnp.float32), axis=(0, 1)) * scale_factor
    dconv_wide = conv_gradient.astype(jnp.float32)
    kern_terms = []
    for row_off in range(7):
        for col_off in range(7):
            window = padded[row_off : row_off + rows, col_off : col_off + cols].astype(jnp.float32)
            kern_terms.append(jnp.sum(dconv_wide * window, axis=(0, 1)))
    grad_kern = jnp.stack(kern_terms, axis=0).reshape(7, 7, chans) * scale_factor
    dpad, north, south = sphere_pad(conv_gradient)
    zero_rows = jnp.zeros((3, cols + 6, chans), jnp.bfloat16)
    inner = jnp.concatenate(
        [jnp.where(north, zero_rows, dpad[:3]), dpad[3:-3], jnp.where(south, zero_rows, dpad[-3:])],
        axis=0,
    )
    spacer = jnp.zeros((6, cols + 6, chans), jnp.bfloat16)
    fold_north = jnp.concatenate([jnp.where(north, dpad[:3], zero_rows), spacer], axis=0)
    fold_south = jnp.concatenate([spacer, jnp.where(south, dpad[-3:], zero_rows)], axis=0)
    adjoint = jnp.zeros((rows, cols, chans), jnp.float32)
    north_term = jnp.zeros((3, cols, chans), jnp.float32)
    south_term = jnp.zeros((3, cols, chans), jnp.float32)
    for row_off in range(7):
        for col_off in range(7):
            weight = weights[row_off, col_off]
            col_from = 6 - col_off
            adjoint = adjoint + weight * inner[
                6 - row_off : 6 - row_off + rows, col_from : col_from + cols
            ].astype(jnp.float32)
            north_term = north_term + weight * fold_north[
                row_off : row_off + 3, col_from : col_from + cols
            ].astype(jnp.float32)
            south_term = south_term + weight * fold_south[
                row_off : row_off + 3, col_from : col_from + cols
            ].astype(jnp.float32)
    adjoint = adjoint.at[:3].add(north_term)
    adjoint = adjoint.at[rows - 3 :].add(south_term)
    grad_fields = (cotangent.astype(jnp.float32) + adjoint).astype(jnp.bfloat16)
    sum_kern, sum_dwb, sum_gn, sum_sh, sum_exp, sum_bexp, sum_proj, sum_bproj = lax.psum(
        (grad_kern, grad_dwb, gain_gradient, grad_sh, grad_exp, grad_bexp, grad_proj, grad_bproj),
        ("lon", "lat"),
    )
    return (
        block_out,
        grad_fields,
        sum_kern,
        sum_dwb,
        sum_gn,
        sum_sh,
        sum_exp,
        sum_bexp,
        sum_proj,
        sum_bproj,
    )


def solution(mesh):
    placed = (P("lat", "lon", None), P("lat", "lon", None), P(), P(), P(), P(), P(), P(), P(), P())
    return jax.shard_map(
        local,
        mesh=mesh,
        in_specs=placed,
        out_specs=(
            P("lat", "lon", None),
            P("lat", "lon", None),
            P(),
            P(),
            P(),
            P(),
            P(),
            P(),
            P(),
            P(),
        ),
        check_vma=False,
    )
```

profile of v0, /device:TPU:0, one launch (start us, length us, event | category | flops | bytes accessed | tf_op | source)
XLA Modules:
  0.0 221.7 jit_solution(7986544816358134473)
XLA Ops:
  7.2 1.1 fusion.150
  8.4 3.0 %collective-permute-start = (bf16[32,3,256]{2,1,0:T(4,128)(2,1)S(1)}, bf16[32,3,256]{2,1,0:T(4,128)(2,1)S(1)}, u32[]{:S(2)}, u32[]{:S(2)}) collective-permute-start(bf16[32,3,256]{2,1,0:T(4,128)(2,1)S(1)} %get-tuple-element.121), channel_id=1, source_target_pairs={{0,4},{4,8},{8,12},{12,16},{16,20},{20,24},{24,28},{28,0},{1,5},{5... | collective-permute-start | bytes 147464 | tf_op jit(solution)/shard_map/ppermute | solution.py:17
  11.4 3.1 %collective-permute-start.1 = (bf16[32,3,256]{2,1,0:T(4,128)(2,1)S(1)}, bf16[32,3,256]{2,1,0:T(4,128)(2,1)S(1)}, u32[]{:S(2)}, u32[]{:S(2)}) collective-permute-start(bf16[32,3,256]{2,1,0:T(4,128)(2,1)S(1)} %get-tuple-element.122), channel_id=1, source_target_pairs={{4,0},{8,4},{12,8},{16,12},{20,16},{24,20},{28,24},{0,28},{5,1},{9... | collective-permute-start | bytes 147464 | tf_op jit(solution)/shard_map/ppermute | solution.py:18
  14.5 1.0 fusion.151
  15.5 1.0 fusion.152
  21.6 1.1 constant_dynamic-update-slice_fusion.1
  25.3 1.2 convert_element_type.582
  27.4 1.5 collective-permute-start.3
  28.9 1.3 collective-permute-start.4
  31.1 4.3 %collective-permute-done.2 = bf16[3,38,256]{2,1,0:T(8,128)(2,1)S(1)} collective-permute-done((bf16[3,38,256]{2,1,0:T(8,128)(2,1)S(1)}, bf16[3,38,256]{2,1,0:T(8,128)(2,1)S(1)}, u32[]{:S(2)}, u32[]{:S(2)}) %collective-permute-start.2) | collective-permute-done | bytes 58400 | tf_op jit(solution)/shard_map/ppermute | solution.py:26
  35.9 8.6 %add_reduce_fusion = (f32[32,32]{1,0:T(8,128)S(1)}, f32[32,32,256]{2,1,0:T(8,128)}) fusion(f32[256]{0:T(256)S(1)} %convert_element_type.576, bf16[35,38,256]{2,1,0:T(8,128)(2,1)S(1)} %get-tuple-element.114, f32[256]{0:T(256)S(1)} %bitcast.258, f32[256]{0:T(256)S(1)} %bitcast.254, f32[256]{0:T(256)S(1)} %bitcast.250, f32[256]{0:T(256)S(1)} %bitcast.246, ...), kind=kLoop, calls=%fused_computation.247 | loop fusion | flops 41155584 | bytes 25270272 | tf_op jit(solution)/shard_map/reduce_sum | solution.py:80
  44.5 1.6 multiply_reduce_fusion.2
  46.2 1.6 fusion.132
  47.8 1.2 multiply_convert_fusion
  49.0 2.5 %convert_reduce_fusion = (f32[1024]{0:T(1024)S(1)}, bf16[1024,1024]{1,0:T(8,128)(2,1)S(1)}) fusion(f32[1024,1024]{1,0:T(8,128)S(1)} %get-tuple-element.181, f32[1024]{0:T(1024)S(1)} %convert_element_type.580, bf16[1024,256]{1,0:T(8,128)(2,1)S(1)} %bitcast.175, bf16[1024,256]{1,0:T(8,128)(2,1)S(1)} %copy-done.22), kind=kOutput, calls=%fused_computation.57 | convolution fusion | flops 550501376 | bytes 7348224 | tf_op jit(solution)/shard_map/dot_general | solution.py:103
  51.5 1.7 convolution_multiply_fusion.1
  53.3 1.4 multiply_reduce_fusion
  55.6 3.2 %fusion.130 = (f32[256]{0:T(256)S(1)}, f32[256]{0:T(256)S(1)}, f32[256]{0:T(256)S(1)}, f32[256]{0:T(256)S(1)}, f32[256]{0:T(256)S(1)}, /*index=5*/f32[256]{0:T(2...) fusion(bf16[35,38,256]{2,1,0:T(8,128)(2,1)S(1)} %get-tuple-elem, ...), kind=kLoop, calls=%fused_computation.237 | loop fusion | flops 14413312 | bytes 9979904 | tf_op jit(solution)/shard_map/reduce_sum | solution.py:123
  58.8 3.2 %fusion.102 = (f32[256]{0:T(256)}, f32[256]{0:T(256)}, f32[256]{0:T(256)}, f32[256]{0:T(256)}, f32[256]{0:T(256)}, /*index=5*/f32[256]{0:T(256)}, f32[256]{0:T(2...) fusion(bf16[35,38,256]{2,1,0:T(8,128)(2,1)S(1)} %get-tuple-elem, ...), kind=kLoop, calls=%fused_computation.209 | loop fusion | flops 14413312 | bytes 9979904 | tf_op jit(solution)/shard_map/reduce_sum | solution.py:123
  62.1 1.7 convolution_multiply_fusion
  63.8 3.5 %fusion.112 = (f32[256]{0:T(256)S(1)}, f32[256]{0:T(256)S(1)}, f32[256]{0:T(256)S(1)}, f32[256]{0:T(256)S(1)}, f32[256]{0:T(256)S(1)}, /*index=5*/f32[256]{0:T(2...) fusion(bf16[35,38,256]{2,1,0:T(8,128)(2,1)S(1)} %get-tuple-elem, ...), kind=kLoop, calls=%fused_computation.219 | loop fusion | flops 12841728 | bytes 5829632 | tf_op jit(solution)/shard_map/reduce_sum | solution.py:123
  67.4 4.4 %stack.199 = f32[49,256]{1,0:T(8,128)S(1)} concatenate(f32[1,256]{1,0:T(1,128)S(1)} %bitcast.376, f32[1,256]{1,0:T(1,128)S(1)} %bitcast.377, f32[1,256]{1,0:T(1,128)S(1)} %bitcast.378, f32[1,256]{1,0:T(1,128)} %bitcast.421, f32[1,256]{1,0:T(1,128)} %bitcast.420, f32[1,256]{1,0:T(1,128)} %bitcast.419, f32[1,256]{1,0:T(1,128)} %bitcast.418, f32[1,256]{1,0:T(1,128)} %bitcast.417, ...), dimensions={0} | concatenate | bytes 100352 | tf_op jit(solution)/shard_map/stack | solution.py:124
  71.9 4.7 %collective-permute-start.6 = (bf16[32,3,256]{2,1,0:T(4,128)(2,1)S(1)}, bf16[32,3,256]{2,1,0:T(4,128)(2,1)S(1)}, u32[]{:S(2)}, u32[]{:S(2)}) collective-permute-start(bf16[32,3,256]{2,1,0:T(4,128)(2,1)S(1)} %get-tuple-element.119), channel_id=1, source_target_pairs={{4,0},{8,4},{12,8},{16,12},{20,16},{24,20},{28,24},{0,28},{5,1},{9... | collective-permute-start | bytes 147464 | tf_op jit(solution)/shard_map/ppermute | solution.py:18
  76.7 3.1 %fusion.7 = bf16[1024,256]{1,0:T(8,128)(2,1)} fusion(bf16[1024,1024]{1,0:T(8,128)(2,1)} %copy-done.4, bf16[1024,256]{1,0:T(8,128)(2,1)S(1)} %copy-done.23, f32[256]{0:T(256)S(1)} %copy-done.24, bf16[1024,256]{1,0:T(8,128)(2,1)S(1)} %bitcast.174), kind=kOutput, calls=%fused_computation.114 | convolution fusion | flops 537919488 | bytes 3671040 | tf_op jit(solution)/shard_map/dot_general | solution.py:93
  79.8 1.3 collective-permute-start.8
  81.2 3.7 %collective-permute-start.9 = (bf16[3,38,256]{2,1,0:T(8,128)(2,1)S(1)}, bf16[3,38,256]{2,1,0:T(8,128)(2,1)S(1)}, u32[]{:S(2)}, u32[]{:S(2)}) collective-permute-start(bf16[3,38,256]{2,1,0:T(8,128)(2,1)S(1)} %get-tuple-element.112), channel_id=1, source_target_pairs={{0,1},{1,2},{2,3},{4,5},{5,6},{6,7},{8,9},{9,10},{10,11},{12,13},{... | collective-permute-start | bytes 175112 | tf_op jit(solution)/shard_map/ppermute | solution.py:17
  85.0 6.9 %collective-permute-done.7 = bf16[3,38,256]{2,1,0:T(8,128)(2,1)S(1)} collective-permute-done((bf16[3,38,256]{2,1,0:T(8,128)(2,1)S(1)}, bf16[3,38,256]{2,1,0:T(8,128)(2,1)S(1)}, u32[]{:S(2)}, u32[]{:S(2)}) %collective-permute-start.7) | collective-permute-done | bytes 58400 | tf_op jit(solution)/shard_map/ppermute | solution.py:26
  92.5 8.0 %fusion.81 = f32[32,32,256]{2,1,0:T(8,128)S(1)} fusion(bf16[32,32,256]{2,1,0:T(8,128)(2,1)S(1)} %bitcast.173, bf16[32,3,256]{2,1,0:T(4,128)(2,1)S(1)} %collective-permute-done.5, bf16[32,3,256]{2,1,0:T(4,128)(2,1)S(1)} %collective-permute-done.6, bf16[35,38,256]{2,1,0:T(8,128)(2,1)S(1)} %get-tuple-element.110, ...), kind=kLoop, calls=%fused_computation.188 | loop fusion | flops 42991616 | bytes 23741440 | tf_op jit(solution)/shard_map/add | solution.py:141
  101.3 1.1 convert_reduce_fusion.1
  102.3 41.5 %all-reduce.2 = (f32[7,7,256]{2,1,0:T(8,128)}, f32[256]{0:T(256)}, f32[256]{0:T(256)}, f32[256]{0:T(256)}, f32[1024]{0:T(1024)}, /*index=5*/f32[256]{0:T(256)}) all-reduce(f32[7,7,256]{2,1,0:T(8,128)S(1)} %mul.2248, f32[256]{0:T(256)S(1)} %broadcast_multiply_fusion.8, ...), channel_id=1, replica_groups=mesh['lon'=8,'lat'=4] {'lon','lat'}, use_global_device_ids=true, to_apply=%region_53.54 | all-reduce | flops 14592 | bytes 116736 | tf_op jit(solution)/shard_map/psum | solution.py:153
  143.8 67.6 %all-reduce.6.cloned.1.call-done = (f32[256,1024]{1,0:T(8,128)}, f32[1024,256]{1,0:T(8,128)}) async-done(((f32[256,1024]{1,0:T(8,128)}, f32[1024,256]{1,0:T(8,128)}), (f32[256,1024]{1,0:T(8,128)}, f32[1024,256]{1,0:T(8,128)})) %all-reduce.6.cloned.1.call-update) | async-done | bytes 2097168 | tf_op jit(solution)/shard_map/psum | solution.py:153
  211.5 2.4 %copy.25 = f32[256,1024]{1,0:T(8,128)} copy(f32[256,1024]{1,0:T(8,128)} %get-tuple-element.223) | data formatting | bytes 2097152
  (108 shorter events, 13.4 us)
Async XLA Ops:
  7.2 40.6 %copy-start = (bf16[256,1024]{1,0:T(8,128)(2,1)S(1)}, bf16[256,1024]{1,0:T(8,128)(2,1)}, u32[]{:S(2)}) copy-start(bf16[256,1024]{1,0:T(8,128)(2,1)} %param.20) | copy-start | bytes 1572868
  7.2 28.3 %copy-start.2 = (bf16[32,32,256]{2,1,0:T(8,128)(2,1)S(1)}, bf16[32,32,256]{2,1,0:T(8,128)(2,1)}, u32[]{:S(2)}) copy-start(bf16[32,32,256]{2,1,0:T(8,128)(2,1)} %param.14) | copy-start | bytes 1572868
  7.2 204.3 %all-reduce.6.cloned.1.call-start = ((), (), s32[]{:S(2)}) async-start(), calls=%async_computation | async-start | bytes 4194304 | tf_op jit(solution)/shard_map/psum | solution.py:153
  8.4 18.2 %collective-permute-start = (bf16[32,3,256]{2,1,0:T(4,128)(2,1)S(1)}, bf16[32,3,256]{2,1,0:T(4,128)(2,1)S(1)}, u32[]{:S(2)}, u32[]{:S(2)}) collective-permute-start(bf16[32,3,256]{2,1,0:T(4,128)(2,1)S(1)} %get-tuple-element.121), channel_id=1, source_target_pairs={{0,4},{4,8},{8,12},{12,16},{16,20},{20,24},{24,28},{28,0},{1,5},{5... | collective-permute-start | bytes 147464 | tf_op jit(solution)/shard_map/ppermute | solution.py:17
  11.4 15.2 %collective-permute-start.1 = (bf16[32,3,256]{2,1,0:T(4,128)(2,1)S(1)}, bf16[32,3,256]{2,1,0:T(4,128)(2,1)S(1)}, u32[]{:S(2)}, u32[]{:S(2)}) collective-permute-start(bf16[32,3,256]{2,1,0:T(4,128)(2,1)S(1)} %get-tuple-element.122), channel_id=1, source_target_pairs={{4,0},{8,4},{12,8},{16,12},{20,16},{24,20},{28,24},{0,28},{5,1},{9... | collective-permute-start | bytes 147464 | tf_op jit(solution)/shard_map/ppermute | solution.py:18
  27.4 8.0 %collective-permute-start.3 = (bf16[3,38,256]{2,1,0:T(8,128)(2,1)S(1)}, bf16[3,38,256]{2,1,0:T(8,128)(2,1)S(1)}, u32[]{:S(2)}, u32[]{:S(2)}) collective-permute-start(bf16[3,38,256]{2,1,0:T(8,128)(2,1)S(1)} %get-tuple-element.116), channel_id=1, source_target_pairs={{0,1},{1,2},{2,3},{4,5},{5,6},{6,7},{8,9},{9,10},{10,11},{12,13},{... | collective-permute-start | bytes 175112 | tf_op jit(solution)/shard_map/ppermute | solution.py:17
  28.9 6.5 %collective-permute-start.4 = (bf16[3,38,256]{2,1,0:T(8,128)(2,1)S(1)}, bf16[3,38,256]{2,1,0:T(8,128)(2,1)S(1)}, u32[]{:S(2)}, u32[]{:S(2)}) collective-permute-start(bf16[3,38,256]{2,1,0:T(8,128)(2,1)S(1)} %get-tuple-element.115), channel_id=1, source_target_pairs={{1,0},{2,1},{3,2},{5,4},{6,5},{7,6},{9,8},{10,9},{11,10},{13,12},{... | collective-permute-start | bytes 175112 | tf_op jit(solution)/shard_map/ppermute | solution.py:18
  30.2 5.2 %collective-permute-start.2 = (bf16[3,38,256]{2,1,0:T(8,128)(2,1)S(1)}, bf16[3,38,256]{2,1,0:T(8,128)(2,1)S(1)}, u32[]{:S(2)}, u32[]{:S(2)}) collective-permute-start(bf16[3,38,256]{2,1,0:T(8,128)(2,1)S(1)} %reverse_select_fusion.1), channel_id=1, source_target_pairs={{0,16},{4,20},{8,24},{12,28},{16,0},{20,4},{24,8},{28,12},{1,17},{... | collective-permute-start | bytes 175112 | tf_op jit(solution)/shard_map/ppermute | solution.py:26
  49.0 13.1 %copy-start.4 = (bf16[1024,1024]{1,0:T(8,128)(2,1)}, bf16[1024,1024]{1,0:T(8,128)(2,1)S(1)}, u32[]{:S(2)}) copy-start(bf16[1024,1024]{1,0:T(8,128)(2,1)S(1)} %get-tuple-element.180) | copy-start | bytes 6291460
  67.3 9.3 %copy-start.3 = (bf16[32,32,256]{2,1,0:T(8,128)(2,1)S(1)}, bf16[32,32,256]{2,1,0:T(8,128)(2,1)}, u32[]{:S(2)}) copy-start(bf16[32,32,256]{2,1,0:T(8,128)(2,1)} %param.14) | copy-start | bytes 1572868
  67.3 9.3 %copy-start.23 = (bf16[1024,256]{1,0:T(8,128)(2,1)S(1)}, bf16[1024,256]{1,0:T(8,128)(2,1)}, u32[]{:S(2)}) copy-start(bf16[1024,256]{1,0:T(8,128)(2,1)} %param.22) | copy-start | bytes 1572868
  67.4 9.3 %copy-start.24 = (f32[256]{0:T(256)S(1)}, f32[256]{0:T(256)}, u32[]{:S(2)}) copy-start(f32[256]{0:T(256)} %convert_element_type.582) | copy-start | bytes 3076
  71.8 8.0 %collective-permute-start.5 = (bf16[32,3,256]{2,1,0:T(4,128)(2,1)S(1)}, bf16[32,3,256]{2,1,0:T(4,128)(2,1)S(1)}, u32[]{:S(2)}, u32[]{:S(2)}) collective-permute-start(bf16[32,3,256]{2,1,0:T(4,128)(2,1)S(1)} %get-tuple-element.120), channel_id=1, source_target_pairs={{0,4},{4,8},{8,12},{12,16},{16,20},{20,24},{24,28},{28,0},{1,5},{5... | collective-permute-start | bytes 147464 | tf_op jit(solution)/shard_map/ppermute | solution.py:17
  71.9 7.9 %collective-permute-start.6 = (bf16[32,3,256]{2,1,0:T(4,128)(2,1)S(1)}, bf16[32,3,256]{2,1,0:T(4,128)(2,1)S(1)}, u32[]{:S(2)}, u32[]{:S(2)}) collective-permute-start(bf16[32,3,256]{2,1,0:T(4,128)(2,1)S(1)} %get-tuple-element.119), channel_id=1, source_target_pairs={{4,0},{8,4},{12,8},{16,12},{20,16},{24,20},{28,24},{0,28},{5,1},{9... | collective-permute-start | bytes 147464 | tf_op jit(solution)/shard_map/ppermute | solution.py:18
  76.6 3.1 %copy-start.20 = (f32[256]{0:T(256)S(1)}, f32[256]{0:T(256)}, u32[]{:S(2)}) copy-start(f32[256]{0:T(256)} %get-tuple-element.34) | copy-start | bytes 3076
  76.6 3.1 %copy-start.21 = (f32[256]{0:T(256)S(1)}, f32[256]{0:T(256)}, u32[]{:S(2)}) copy-start(f32[256]{0:T(256)} %get-tuple-element.85) | copy-start | bytes 3076
  79.8 12.1 %collective-permute-start.8 = (bf16[3,38,256]{2,1,0:T(8,128)(2,1)S(1)}, bf16[3,38,256]{2,1,0:T(8,128)(2,1)S(1)}, u32[]{:S(2)}, u32[]{:S(2)}) collective-permute-start(bf16[3,38,256]{2,1,0:T(8,128)(2,1)S(1)} %get-tuple-element.111), channel_id=1, source_target_pairs={{1,0},{2,1},{3,2},{5,4},{6,5},{7,6},{9,8},{10,9},{11,10},{13,12},{... | collective-permute-start | bytes 175112 | tf_op jit(solution)/shard_map/ppermute | solution.py:18
  81.2 10.7 %collective-permute-start.9 = (bf16[3,38,256]{2,1,0:T(8,128)(2,1)S(1)}, bf16[3,38,256]{2,1,0:T(8,128)(2,1)S(1)}, u32[]{:S(2)}, u32[]{:S(2)}) collective-permute-start(bf16[3,38,256]{2,1,0:T(8,128)(2,1)S(1)} %get-tuple-element.112), channel_id=1, source_target_pairs={{0,1},{1,2},{2,3},{4,5},{5,6},{6,7},{8,9},{9,10},{10,11},{12,13},{... | collective-permute-start | bytes 175112 | tf_op jit(solution)/shard_map/ppermute | solution.py:17
  84.8 7.1 %collective-permute-start.7 = (bf16[3,38,256]{2,1,0:T(8,128)(2,1)S(1)}, bf16[3,38,256]{2,1,0:T(8,128)(2,1)S(1)}, u32[]{:S(2)}, u32[]{:S(2)}) collective-permute-start(bf16[3,38,256]{2,1,0:T(8,128)(2,1)S(1)} %reverse_select_fusion), channel_id=1, source_target_pairs={{0,16},{4,20},{8,24},{12,28},{16,0},{20,4},{24,8},{28,12},{1,17},{... | collective-permute-start | bytes 175112 | tf_op jit(solution)/shard_map/ppermute | solution.py:26
  92.3 8.2 %copy-start.8 = (f32[256]{0:T(256)S(1)}, f32[256]{0:T(256)}, u32[]{:S(2)}) copy-start(f32[256]{0:T(256)} %get-tuple-element.200) | copy-start | bytes 3076
  92.3 8.2 %copy-start.9 = (f32[256]{0:T(256)S(1)}, f32[256]{0:T(256)}, u32[]{:S(2)}) copy-start(f32[256]{0:T(256)} %get-tuple-element.189) | copy-start | bytes 3076
  92.4 8.2 %copy-start.10 = (f32[256]{0:T(256)S(1)}, f32[256]{0:T(256)}, u32[]{:S(2)}) copy-start(f32[256]{0:T(256)} %get-tuple-element.190) | copy-start | bytes 3076
  92.4 8.2 %copy-start.11 = (f32[256]{0:T(256)S(1)}, f32[256]{0:T(256)}, u32[]{:S(2)}) copy-start(f32[256]{0:T(256)} %get-tuple-element.191) | copy-start | bytes 3076
  92.4 8.2 %copy-start.12 = (f32[256]{0:T(256)S(1)}, f32[256]{0:T(256)}, u32[]{:S(2)}) copy-start(f32[256]{0:T(256)} %get-tuple-element.192) | copy-start | bytes 3076
  92.4 8.2 %copy-start.13 = (f32[256]{0:T(256)S(1)}, f32[256]{0:T(256)}, u32[]{:S(2)}) copy-start(f32[256]{0:T(256)} %get-tuple-element.193) | copy-start | bytes 3076
  92.4 8.2 %copy-start.14 = (f32[256]{0:T(256)S(1)}, f32[256]{0:T(256)}, u32[]{:S(2)}) copy-start(f32[256]{0:T(256)} %get-tuple-element.194) | copy-start | bytes 3076
  92.4 8.2 %copy-start.15 = (f32[256]{0:T(256)S(1)}, f32[256]{0:T(256)}, u32[]{:S(2)}) copy-start(f32[256]{0:T(256)} %get-tuple-element.195) | copy-start | bytes 3076
  92.4 8.2 %copy-start.16 = (f32[256]{0:T(256)S(1)}, f32[256]{0:T(256)}, u32[]{:S(2)}) copy-start(f32[256]{0:T(256)} %get-tuple-element.196) | copy-start | bytes 3076
  92.4 8.2 %copy-start.17 = (f32[256]{0:T(256)S(1)}, f32[256]{0:T(256)}, u32[]{:S(2)}) copy-start(f32[256]{0:T(256)} %get-tuple-element.197) | copy-start | bytes 3076
  92.4 8.2 %copy-start.18 = (f32[256]{0:T(256)S(1)}, f32[256]{0:T(256)}, u32[]{:S(2)}) copy-start(f32[256]{0:T(256)} %get-tuple-element.198) | copy-start | bytes 3076
  92.5 8.6 %copy-start.19 = (f32[256]{0:T(256)S(1)}, f32[256]{0:T(256)}, u32[]{:S(2)}) copy-start(f32[256]{0:T(256)} %fusion.147) | copy-start | bytes 3076
  92.5 8.8 %copy-start.7 = (bf16[32,32,256]{2,1,0:T(8,128)(2,1)S(1)}, bf16[32,32,256]{2,1,0:T(8,128)(2,1)}, u32[]{:S(2)}) copy-start(bf16[32,32,256]{2,1,0:T(8,128)(2,1)} %param.15) | copy-start | bytes 1572868
  (4 other events, 6.2 us)
Sparse Core Ops, SparseCore 0:
  76.7 134.6 all-reduce.5
where the time goes:
time: 223 us; the launch traced here: 222 us
  waiting for transfers between devices  78.9 us (35%)
  other arithmetic  42.2 us (19%)
  blocking collectives  41.5 us (19%)
  starting transfers between devices  19.5 us (9%)
  between operations  14.7 us (7%)
  local copies, waits for them, and re-layouts  13.3 us (6%)
  matrix products  11.6 us (5%)
    psum x1, waiting for transfers between devices, local(): lax.psum((grad_kern, grad_dwb, gain_gradient, grad_sh, grad_exp, grad_bex...  67.6 us
    psum x1, blocking collectives, local(): lax.psum((grad_kern, grad_dwb, gain_gradient, grad_sh, grad_exp, grad_bex...  41.5 us
    ppermute x2, waiting for transfers between devices, from_behind(): return lax.ppermute(value, axis, pairs)  11.3 us
    ppermute x4, starting transfers between devices, extended(): after = lax.ppermute(first, axis, down)  10.4 us
    reduce_sum x3, other arithmetic, local(): kern_terms.append(jnp.sum(dconv_wide * window, axis=(0, 1)))  10 us
    reduce_sum x1, other arithmetic, local(): mean_removed = conv - jnp.mean(conv, axis=-1, keepdims=True)  8.57 us
    ppermute x4, starting transfers between devices, extended(): before = lax.ppermute(last, axis, up)  8.18 us
    add x1, other arithmetic, local(): adjoint + weight * inner[6 - row_off:6 - row_off + rows, col_from:col_fro...  8.02 us
  transfers between devices with their start and end apart: 11, of which 3 were waited for; matrix products, arithmetic and copies ran while one was open for 11% of the time, Pallas kernels for 0%

commit v1 on v0

--- a/solution.py
+++ b/solution.py
@@ -151,8 +151,20 @@
     adjoint = adjoint.at[rows - 3 :].add(south_term)
     grad_fields = (cotangent.astype(jnp.float32) + adjoint).astype(jnp.bfloat16)
     sum_kern, sum_dwb, sum_gn, sum_sh, sum_exp, sum_bexp, sum_proj, sum_bproj = lax.psum(
-        (grad_kern, grad_dwb, gain_gradient, grad_sh, grad_exp, grad_bexp, grad_proj, grad_bproj),
-        ("lon", "lat"),
+        lax.psum(
+            (
+                grad_kern,
+                grad_dwb,
+                gain_gradient,
+                grad_sh,
+                grad_exp,
+                grad_bexp,
+                grad_proj,
+                grad_bproj,
+            ),
+            "lat",
+        ),
+        "lon",
     )
     return (
         block_out,

time: 223 us -> 247 us (1.11)
  waiting for transfers between devices: 78.9 us -> 94.3 us
  blocking collectives: 41.5 us -> 50.8 us
    psum x0 -> x1, waiting for transfers between devices: none -> 46.3 us  [local(): lax.psum(lax.psum((grad_kern, grad_dwb, gain_gradient, grad_sh, grad_exp,...]
    psum x0 -> x1, blocking collectives: none -> 39.3 us  [local(): lax.psum(lax.psum((grad_kern, grad_dwb, gain_gradient, grad_sh, grad_exp,...]
    psum x1, blocking collectives: 41.5 us -> 11.5 us  [local(): lax.psum((grad_kern, grad_dwb, gain_gradient, grad_sh, grad_exp, grad_bex...]
    psum x1, waiting for transfers between devices: 67.6 us -> 37.9 us  [local(): lax.psum((grad_kern, grad_dwb, gain_gradient, grad_sh, grad_exp, grad_bex...]
  transfers between devices with their start and end apart: 11 -> 12, of which waited for: 3 -> 4; matrix products, arithmetic and copies ran while one was open for 11% -> 10% of each run, Pallas kernels for 0% -> 0%
where the time goes in v1:
time: 247 us
  waiting for transfers between devices  94.3 us (38%)
  blocking collectives  50.8 us (21%)
  other arithmetic  42.2 us (17%)
  starting transfers between devices  19.7 us (8%)
  between operations  14.7 us (6%)
  local copies, waits for them, and re-layouts  13.3 us (5%)
  matrix products  11.6 us (5%)
    psum x1, waiting for transfers between devices, local(): lax.psum(lax.psum((grad_kern, grad_dwb, gain_gradient, grad_sh, grad_exp,...  46.3 us
    psum x1, blocking collectives, local(): lax.psum(lax.psum((grad_kern, grad_dwb, gain_gradient, grad_sh, grad_exp,...  39.3 us
    psum x1, waiting for transfers between devices, local(): lax.psum((grad_kern, grad_dwb, gain_gradient, grad_sh, grad_exp, grad_bex...  37.9 us
    psum x1, blocking collectives, local(): lax.psum((grad_kern, grad_dwb, gain_gradient, grad_sh, grad_exp, grad_bex...  11.5 us
    ppermute x4, starting transfers between devices, extended(): after = lax.ppermute(first, axis, down)  10.4 us
    reduce_sum x3, other arithmetic, local(): kern_terms.append(jnp.sum(dconv_wide * window, axis=(0, 1)))  10.1 us
    ppermute x2, waiting for transfers between devices, from_behind(): return lax.ppermute(value, axis, pairs)  10.1 us
    reduce_sum x1, other arithmetic, local(): mean_removed = conv - jnp.mean(conv, axis=-1, keepdims=True)  8.57 us
  transfers between devices with their start and end apart: 12, of which 4 were waited for; matrix products, arithmetic and copies ran while one was open for 10% of the time, Pallas kernels for 0%

profile of v1, /device:TPU:0, one launch (start us, length us, event | category | flops | bytes accessed | tf_op | source)
XLA Modules:
  0.0 246.6 jit_solution(3287491690525516946)
XLA Ops:
  7.2 1.1 fusion.150
  8.4 3.0 %collective-permute-start = (bf16[32,3,256]{2,1,0:T(4,128)(2,1)S(1)}, bf16[32,3,256]{2,1,0:T(4,128)(2,1)S(1)}, u32[]{:S(2)}, u32[]{:S(2)}) collective-permute-start(bf16[32,3,256]{2,1,0:T(4,128)(2,1)S(1)} %get-tuple-element.129), channel_id=1, source_target_pairs={{0,4},{4,8},{8,12},{12,16},{16,20},{20,24},{24,28},{28,0},{1,5},{5... | collective-permute-start | bytes 147464 | tf_op jit(solution)/shard_map/ppermute | solution.py:17
  11.4 3.1 %collective-permute-start.1 = (bf16[32,3,256]{2,1,0:T(4,128)(2,1)S(1)}, bf16[32,3,256]{2,1,0:T(4,128)(2,1)S(1)}, u32[]{:S(2)}, u32[]{:S(2)}) collective-permute-start(bf16[32,3,256]{2,1,0:T(4,128)(2,1)S(1)} %get-tuple-element.130), channel_id=1, source_target_pairs={{4,0},{8,4},{12,8},{16,12},{20,16},{24,20},{28,24},{0,28},{5,1},{9... | collective-permute-start | bytes 147464 | tf_op jit(solution)/shard_map/ppermute | solution.py:18
  21.6 1.1 constant_dynamic-update-slice_fusion.1
  25.3 1.2 convert_element_type.582
  27.4 1.5 collective-permute-start.3
  28.9 1.3 collective-permute-start.4
  31.1 4.3 %collective-permute-done.2 = bf16[3,38,256]{2,1,0:T(8,128)(2,1)S(1)} collective-permute-done((bf16[3,38,256]{2,1,0:T(8,128)(2,1)S(1)}, bf16[3,38,256]{2,1,0:T(8,128)(2,1)S(1)}, u32[]{:S(2)}, u32[]{:S(2)}) %collective-permute-start.2) | collective-permute-done | bytes 58400 | tf_op jit(solution)/shard_map/ppermute | solution.py:26
  35.9 8.6 %add_reduce_fusion = (f32[32,32]{1,0:T(8,128)S(1)}, f32[32,32,256]{2,1,0:T(8,128)}) fusion(f32[256]{0:T(256)S(1)} %convert_element_type.576, bf16[35,38,256]{2,1,0:T(8,128)(2,1)S(1)} %get-tuple-element.122, f32[256]{0:T(256)S(1)} %bitcast.258, f32[256]{0:T(256)S(1)} %bitcast.254, f32[256]{0:T(256)S(1)} %bitcast.250, f32[256]{0:T(256)S(1)} %bitcast.246, ...), kind=kLoop, calls=%fused_computation.247 | loop fusion | flops 41155584 | bytes 25270272 | tf_op jit(solution)/shard_map/reduce_sum | solution.py:80
  44.5 1.6 multiply_reduce_fusion.2
  46.2 1.6 fusion.132
  47.8 1.2 multiply_convert_fusion
  49.0 2.5 %convert_reduce_fusion = (f32[1024]{0:T(1024)S(1)}, bf16[1024,1024]{1,0:T(8,128)(2,1)S(1)}) fusion(f32[1024,1024]{1,0:T(8,128)S(1)} %get-tuple-element.189, f32[1024]{0:T(1024)S(1)} %convert_element_type.580, bf16[1024,256]{1,0:T(8,128)(2,1)S(1)} %bitcast.175, bf16[1024,256]{1,0:T(8,128)(2,1)S(1)} %copy-done.22), kind=kOutput, calls=%fused_computation.57 | convolution fusion | flops 550501376 | bytes 7348224 | tf_op jit(solution)/shard_map/dot_general | solution.py:103
  51.5 1.7 convolution_multiply_fusion.1
  53.3 1.4 multiply_reduce_fusion
  55.6 3.2 %fusion.130 = (f32[256]{0:T(256)S(1)}, f32[256]{0:T(256)S(1)}, f32[256]{0:T(256)S(1)}, f32[256]{0:T(256)S(1)}, f32[256]{0:T(256)S(1)}, /*index=5*/f32[256]{0:T(2...) fusion(bf16[35,38,256]{2,1,0:T(8,128)(2,1)S(1)} %get-tuple-elem, ...), kind=kLoop, calls=%fused_computation.237 | loop fusion | flops 14413312 | bytes 9979904 | tf_op jit(solution)/shard_map/reduce_sum | solution.py:123
  58.8 3.2 %fusion.102 = (f32[256]{0:T(256)}, f32[256]{0:T(256)}, f32[256]{0:T(256)}, f32[256]{0:T(256)}, f32[256]{0:T(256)}, /*index=5*/f32[256]{0:T(256)}, f32[256]{0:T(2...) fusion(bf16[35,38,256]{2,1,0:T(8,128)(2,1)S(1)} %get-tuple-elem, ...), kind=kLoop, calls=%fused_computation.209 | loop fusion | flops 14413312 | bytes 9979904 | tf_op jit(solution)/shard_map/reduce_sum | solution.py:123
  62.1 1.7 convolution_multiply_fusion
  63.8 3.6 %fusion.112 = (f32[256]{0:T(256)S(1)}, f32[256]{0:T(256)S(1)}, f32[256]{0:T(256)S(1)}, f32[256]{0:T(256)S(1)}, f32[256]{0:T(256)S(1)}, /*index=5*/f32[256]{0:T(2...) fusion(bf16[35,38,256]{2,1,0:T(8,128)(2,1)S(1)} %get-tuple-elem, ...), kind=kLoop, calls=%fused_computation.219 | loop fusion | flops 12841728 | bytes 5829632 | tf_op jit(solution)/shard_map/reduce_sum | solution.py:123
  67.4 4.4 %stack.199 = f32[49,256]{1,0:T(8,128)S(1)} concatenate(f32[1,256]{1,0:T(1,128)S(1)} %bitcast.376, f32[1,256]{1,0:T(1,128)S(1)} %bitcast.377, f32[1,256]{1,0:T(1,128)S(1)} %bitcast.378, f32[1,256]{1,0:T(1,128)} %bitcast.421, f32[1,256]{1,0:T(1,128)} %bitcast.420, f32[1,256]{1,0:T(1,128)} %bitcast.419, f32[1,256]{1,0:T(1,128)} %bitcast.418, f32[1,256]{1,0:T(1,128)} %bitcast.417, ...), dimensions={0} | concatenate | bytes 100352 | tf_op jit(solution)/shard_map/stack | solution.py:124
  71.9 4.7 %collective-permute-start.6 = (bf16[32,3,256]{2,1,0:T(4,128)(2,1)S(1)}, bf16[32,3,256]{2,1,0:T(4,128)(2,1)S(1)}, u32[]{:S(2)}, u32[]{:S(2)}) collective-permute-start(bf16[32,3,256]{2,1,0:T(4,128)(2,1)S(1)} %get-tuple-element.127), channel_id=1, source_target_pairs={{4,0},{8,4},{12,8},{16,12},{20,16},{24,20},{28,24},{0,28},{5,1},{9... | collective-permute-start | bytes 147464 | tf_op jit(solution)/shard_map/ppermute | solution.py:18
  77.0 3.1 %fusion.7 = bf16[1024,256]{1,0:T(8,128)(2,1)} fusion(bf16[1024,1024]{1,0:T(8,128)(2,1)} %copy-done.4, bf16[1024,256]{1,0:T(8,128)(2,1)S(1)} %copy-done.23, f32[256]{0:T(256)S(1)} %copy-done.24, bf16[1024,256]{1,0:T(8,128)(2,1)S(1)} %bitcast.174), kind=kOutput, calls=%fused_computation.114 | convolution fusion | flops 537919488 | bytes 3671040 | tf_op jit(solution)/shard_map/dot_general | solution.py:93
  80.2 1.3 collective-permute-start.8
  81.5 3.7 %collective-permute-start.9 = (bf16[3,38,256]{2,1,0:T(8,128)(2,1)S(1)}, bf16[3,38,256]{2,1,0:T(8,128)(2,1)S(1)}, u32[]{:S(2)}, u32[]{:S(2)}) collective-permute-start(bf16[3,38,256]{2,1,0:T(8,128)(2,1)S(1)} %get-tuple-element.120), channel_id=1, source_target_pairs={{0,1},{1,2},{2,3},{4,5},{5,6},{6,7},{8,9},{9,10},{10,11},{12,13},{... | collective-permute-start | bytes 175112 | tf_op jit(solution)/shard_map/ppermute | solution.py:17
  85.3 5.7 %collective-permute-done.7 = bf16[3,38,256]{2,1,0:T(8,128)(2,1)S(1)} collective-permute-done((bf16[3,38,256]{2,1,0:T(8,128)(2,1)S(1)}, bf16[3,38,256]{2,1,0:T(8,128)(2,1)S(1)}, u32[]{:S(2)}, u32[]{:S(2)}) %collective-permute-start.7) | collective-permute-done | bytes 58400 | tf_op jit(solution)/shard_map/ppermute | solution.py:26
  91.4 37.9 %all-reduce.11.cloned.1.call-done = (f32[256,1024]{1,0:T(8,128)}, f32[1024,256]{1,0:T(8,128)}) async-done(((f32[256,1024]{1,0:T(8,128)}, f32[1024,256]{1,0:T(8,128)}), (f32[256,1024]{1,0:T(8,128)}, f32[1024,256]{1,0:T(8,128)})) %all-reduce.11.cloned.1.call-update) | async-done | bytes 2097168 | tf_op jit(solution)/shard_map/psum | solution.py:154
  129.5 8.0 %fusion.81 = f32[32,32,256]{2,1,0:T(8,128)S(1)} fusion(bf16[32,32,256]{2,1,0:T(8,128)(2,1)S(1)} %bitcast.173, bf16[32,3,256]{2,1,0:T(4,128)(2,1)S(1)} %collective-permute-done.5, bf16[32,3,256]{2,1,0:T(4,128)(2,1)S(1)} %collective-permute-done.6, bf16[35,38,256]{2,1,0:T(8,128)(2,1)S(1)} %get-tuple-element.118, ...), kind=kLoop, calls=%fused_computation.188 | loop fusion | flops 42991616 | bytes 23741440 | tf_op jit(solution)/shard_map/add | solution.py:141
  138.2 1.1 convert_reduce_fusion.1
  139.3 11.5 %all-reduce.4 = (f32[7,7,256]{2,1,0:T(8,128)S(1)}, f32[256]{0:T(256)S(1)}, f32[256]{0:T(256)S(1)}, f32[256]{0:T(256)S(1)}, f32[1024]{0:T(1024)S(1)}, /*index=5*/f32[256]{0:T(256)S(1)}) all-reduce(f32[7,7,256]{2,1,0:T(8,128)S(1)} %mul.2248, f32[256]{0:T(256)S(1)} %broadcast_multiply_fusion.8, ...), channel_id=1, replica_groups=mesh['lon'=8,'lat'=4] {'lat'}, use_global_device_ids=true, to_apply=%region_53.54 | all-reduce | flops 14592 | bytes 116736 | tf_op jit(solution)/shard_map/psum | solution.py:154
  150.8 39.3 %all-reduce.2 = (f32[7,7,256]{2,1,0:T(8,128)}, f32[256]{0:T(256)}, f32[256]{0:T(256)}, f32[256]{0:T(256)}, f32[1024]{0:T(1024)}, /*index=5*/f32[256]{0:T(256)}) all-reduce(f32[7,7,256]{2,1,0:T(8,128)S(1)} %get-tuple-element.105, f32[256]{0:T(256)S(1)} %get-tuple-element.106, ...), channel_id=1, replica_groups=mesh['lon'=8,'lat'=4] {'lon'}, use_global_device_ids=true, to_apply=%region_54.55 | all-reduce | flops 14592 | bytes 116736 | tf_op jit(solution)/shard_map/psum | solution.py:153
  190.1 46.3 %all-reduce.9.cloned.1.call-done = (f32[256,1024]{1,0:T(8,128)}, f32[1024,256]{1,0:T(8,128)}) async-done(((f32[256,1024]{1,0:T(8,128)}, f32[1024,256]{1,0:T(8,128)}), (f32[256,1024]{1,0:T(8,128)}, f32[1024,256]{1,0:T(8,128)})) %all-reduce.9.cloned.1.call-update) | async-done | bytes 2097168 | tf_op jit(solution)/shard_map/psum | solution.py:153
  236.4 2.4 copy.27
  (112 shorter events, 15.7 us)
Async XLA Ops:
  7.2 40.6 %copy-start = (bf16[256,1024]{1,0:T(8,128)(2,1)S(1)}, bf16[256,1024]{1,0:T(8,128)(2,1)}, u32[]{:S(2)}) copy-start(bf16[256,1024]{1,0:T(8,128)(2,1)} %param.20) | copy-start | bytes 1572868
  7.2 28.3 %copy-start.2 = (bf16[32,32,256]{2,1,0:T(8,128)(2,1)S(1)}, bf16[32,32,256]{2,1,0:T(8,128)(2,1)}, u32[]{:S(2)}) copy-start(bf16[32,32,256]{2,1,0:T(8,128)(2,1)} %param.14) | copy-start | bytes 1572868
  7.2 122.1 %all-reduce.11.cloned.1.call-start = ((), (), s32[]{:S(2)}) async-start(), calls=%async_computation.1 | async-start | bytes 4194304 | tf_op jit(solution)/shard_map/psum | solution.py:154
  8.4 18.2 %collective-permute-start = (bf16[32,3,256]{2,1,0:T(4,128)(2,1)S(1)}, bf16[32,3,256]{2,1,0:T(4,128)(2,1)S(1)}, u32[]{:S(2)}, u32[]{:S(2)}) collective-permute-start(bf16[32,3,256]{2,1,0:T(4,128)(2,1)S(1)} %get-tuple-element.129), channel_id=1, source_target_pairs={{0,4},{4,8},{8,12},{12,16},{16,20},{20,24},{24,28},{28,0},{1,5},{5... | collective-permute-start | bytes 147464 | tf_op jit(solution)/shard_map/ppermute | solution.py:17
  11.4 15.2 %collective-permute-start.1 = (bf16[32,3,256]{2,1,0:T(4,128)(2,1)S(1)}, bf16[32,3,256]{2,1,0:T(4,128)(2,1)S(1)}, u32[]{:S(2)}, u32[]{:S(2)}) collective-permute-start(bf16[32,3,256]{2,1,0:T(4,128)(2,1)S(1)} %get-tuple-element.130), channel_id=1, source_target_pairs={{4,0},{8,4},{12,8},{16,12},{20,16},{24,20},{28,24},{0,28},{5,1},{9... | collective-permute-start | bytes 147464 | tf_op jit(solution)/shard_map/ppermute | solution.py:18
  27.4 8.0 %collective-permute-start.3 = (bf16[3,38,256]{2,1,0:T(8,128)(2,1)S(1)}, bf16[3,38,256]{2,1,0:T(8,128)(2,1)S(1)}, u32[]{:S(2)}, u32[]{:S(2)}) collective-permute-start(bf16[3,38,256]{2,1,0:T(8,128)(2,1)S(1)} %get-tuple-element.124), channel_id=1, source_target_pairs={{0,1},{1,2},{2,3},{4,5},{5,6},{6,7},{8,9},{9,10},{10,11},{12,13},{... | collective-permute-start | bytes 175112 | tf_op jit(solution)/shard_map/ppermute | solution.py:17
  28.9 6.5 %collective-permute-start.4 = (bf16[3,38,256]{2,1,0:T(8,128)(2,1)S(1)}, bf16[3,38,256]{2,1,0:T(8,128)(2,1)S(1)}, u32[]{:S(2)}, u32[]{:S(2)}) collective-permute-start(bf16[3,38,256]{2,1,0:T(8,128)(2,1)S(1)} %get-tuple-element.123), channel_id=1, source_target_pairs={{1,0},{2,1},{3,2},{5,4},{6,5},{7,6},{9,8},{10,9},{11,10},{13,12},{... | collective-permute-start | bytes 175112 | tf_op jit(solution)/shard_map/ppermute | solution.py:18
  30.2 5.2 %collective-permute-start.2 = (bf16[3,38,256]{2,1,0:T(8,128)(2,1)S(1)}, bf16[3,38,256]{2,1,0:T(8,128)(2,1)S(1)}, u32[]{:S(2)}, u32[]{:S(2)}) collective-permute-start(bf16[3,38,256]{2,1,0:T(8,128)(2,1)S(1)} %reverse_select_fusion.1), channel_id=1, source_target_pairs={{0,16},{4,20},{8,24},{12,28},{16,0},{20,4},{24,8},{28,12},{1,17},{... | collective-permute-start | bytes 175112 | tf_op jit(solution)/shard_map/ppermute | solution.py:26
  49.0 13.1 %copy-start.4 = (bf16[1024,1024]{1,0:T(8,128)(2,1)}, bf16[1024,1024]{1,0:T(8,128)(2,1)S(1)}, u32[]{:S(2)}) copy-start(bf16[1024,1024]{1,0:T(8,128)(2,1)S(1)} %get-tuple-element.188) | copy-start | bytes 6291460
  67.4 9.5 %copy-start.3 = (bf16[32,32,256]{2,1,0:T(8,128)(2,1)S(1)}, bf16[32,32,256]{2,1,0:T(8,128)(2,1)}, u32[]{:S(2)}) copy-start(bf16[32,32,256]{2,1,0:T(8,128)(2,1)} %param.14) | copy-start | bytes 1572868
  67.4 9.5 %copy-start.23 = (bf16[1024,256]{1,0:T(8,128)(2,1)S(1)}, bf16[1024,256]{1,0:T(8,128)(2,1)}, u32[]{:S(2)}) copy-start(bf16[1024,256]{1,0:T(8,128)(2,1)} %param.22) | copy-start | bytes 1572868
  67.4 9.5 %copy-start.24 = (f32[256]{0:T(256)S(1)}, f32[256]{0:T(256)}, u32[]{:S(2)}) copy-start(f32[256]{0:T(256)} %convert_element_type.582) | copy-start | bytes 3076
  71.9 8.2 %collective-permute-start.5 = (bf16[32,3,256]{2,1,0:T(4,128)(2,1)S(1)}, bf16[32,3,256]{2,1,0:T(4,128)(2,1)S(1)}, u32[]{:S(2)}, u32[]{:S(2)}) collective-permute-start(bf16[32,3,256]{2,1,0:T(4,128)(2,1)S(1)} %get-tuple-element.128), channel_id=1, source_target_pairs={{0,4},{4,8},{8,12},{12,16},{16,20},{20,24},{24,28},{28,0},{1,5},{5... | collective-permute-start | bytes 147464 | tf_op jit(solution)/shard_map/ppermute | solution.py:17
  71.9 8.2 %collective-permute-start.6 = (bf16[32,3,256]{2,1,0:T(4,128)(2,1)S(1)}, bf16[32,3,256]{2,1,0:T(4,128)(2,1)S(1)}, u32[]{:S(2)}, u32[]{:S(2)}) collective-permute-start(bf16[32,3,256]{2,1,0:T(4,128)(2,1)S(1)} %get-tuple-element.127), channel_id=1, source_target_pairs={{4,0},{8,4},{12,8},{16,12},{20,16},{24,20},{28,24},{0,28},{5,1},{9... | collective-permute-start | bytes 147464 | tf_op jit(solution)/shard_map/ppermute | solution.py:18
  76.7 159.8 %all-reduce.9.cloned.1.call-start = ((), (), s32[]{:S(2)}) async-start(), calls=%async_computation | async-start | bytes 4194304 | tf_op jit(solution)/shard_map/psum | solution.py:153
  76.9 3.1 %copy-start.20 = (f32[256]{0:T(256)S(1)}, f32[256]{0:T(256)}, u32[]{:S(2)}) copy-start(f32[256]{0:T(256)} %get-tuple-element.34) | copy-start | bytes 3076
  80.2 10.8 %collective-permute-start.8 = (bf16[3,38,256]{2,1,0:T(8,128)(2,1)S(1)}, bf16[3,38,256]{2,1,0:T(8,128)(2,1)S(1)}, u32[]{:S(2)}, u32[]{:S(2)}) collective-permute-start(bf16[3,38,256]{2,1,0:T(8,128)(2,1)S(1)} %get-tuple-element.119), channel_id=1, source_target_pairs={{1,0},{2,1},{3,2},{5,4},{6,5},{7,6},{9,8},{10,9},{11,10},{13,12},{... | collective-permute-start | bytes 175112 | tf_op jit(solution)/shard_map/ppermute | solution.py:18
  81.5 9.5 %collective-permute-start.9 = (bf16[3,38,256]{2,1,0:T(8,128)(2,1)S(1)}, bf16[3,38,256]{2,1,0:T(8,128)(2,1)S(1)}, u32[]{:S(2)}, u32[]{:S(2)}) collective-permute-start(bf16[3,38,256]{2,1,0:T(8,128)(2,1)S(1)} %get-tuple-element.120), channel_id=1, source_target_pairs={{0,1},{1,2},{2,3},{4,5},{5,6},{6,7},{8,9},{9,10},{10,11},{12,13},{... | collective-permute-start | bytes 175112 | tf_op jit(solution)/shard_map/ppermute | solution.py:17
  85.1 5.8 %collective-permute-start.7 = (bf16[3,38,256]{2,1,0:T(8,128)(2,1)S(1)}, bf16[3,38,256]{2,1,0:T(8,128)(2,1)S(1)}, u32[]{:S(2)}, u32[]{:S(2)}) collective-permute-start(bf16[3,38,256]{2,1,0:T(8,128)(2,1)S(1)} %reverse_select_fusion), channel_id=1, source_target_pairs={{0,16},{4,20},{8,24},{12,28},{16,0},{20,4},{24,8},{28,12},{1,17},{... | collective-permute-start | bytes 175112 | tf_op jit(solution)/shard_map/ppermute | solution.py:26
  129.3 8.2 %copy-start.8 = (f32[256]{0:T(256)S(1)}, f32[256]{0:T(256)}, u32[]{:S(2)}) copy-start(f32[256]{0:T(256)} %get-tuple-element.208) | copy-start | bytes 3076
  129.3 8.2 %copy-start.9 = (f32[256]{0:T(256)S(1)}, f32[256]{0:T(256)}, u32[]{:S(2)}) copy-start(f32[256]{0:T(256)} %get-tuple-element.197) | copy-start | bytes 3076
  129.3 8.2 %copy-start.10 = (f32[256]{0:T(256)S(1)}, f32[256]{0:T(256)}, u32[]{:S(2)}) copy-start(f32[256]{0:T(256)} %get-tuple-element.198) | copy-start | bytes 3076
  129.4 8.2 %copy-start.11 = (f32[256]{0:T(256)S(1)}, f32[256]{0:T(256)}, u32[]{:S(2)}) copy-start(f32[256]{0:T(256)} %get-tuple-element.199) | copy-start | bytes 3076
  129.4 8.2 %copy-start.12 = (f32[256]{0:T(256)S(1)}, f32[256]{0:T(256)}, u32[]{:S(2)}) copy-start(f32[256]{0:T(256)} %get-tuple-element.200) | copy-start | bytes 3076
  129.4 8.2 %copy-start.13 = (f32[256]{0:T(256)S(1)}, f32[256]{0:T(256)}, u32[]{:S(2)}) copy-start(f32[256]{0:T(256)} %get-tuple-element.201) | copy-start | bytes 3076
  129.4 8.2 %copy-start.14 = (f32[256]{0:T(256)S(1)}, f32[256]{0:T(256)}, u32[]{:S(2)}) copy-start(f32[256]{0:T(256)} %get-tuple-element.202) | copy-start | bytes 3076
  129.4 8.2 %copy-start.15 = (f32[256]{0:T(256)S(1)}, f32[256]{0:T(256)}, u32[]{:S(2)}) copy-start(f32[256]{0:T(256)} %get-tuple-element.203) | copy-start | bytes 3076
  129.4 8.2 %copy-start.16 = (f32[256]{0:T(256)S(1)}, f32[256]{0:T(256)}, u32[]{:S(2)}) copy-start(f32[256]{0:T(256)} %get-tuple-element.204) | copy-start | bytes 3076
  129.4 8.2 %copy-start.17 = (f32[256]{0:T(256)S(1)}, f32[256]{0:T(256)}, u32[]{:S(2)}) copy-start(f32[256]{0:T(256)} %get-tuple-element.205) | copy-start | bytes 3076
  129.4 8.2 %copy-start.18 = (f32[256]{0:T(256)S(1)}, f32[256]{0:T(256)}, u32[]{:S(2)}) copy-start(f32[256]{0:T(256)} %get-tuple-element.206) | copy-start | bytes 3076
  129.4 8.6 %copy-start.19 = (f32[256]{0:T(256)S(1)}, f32[256]{0:T(256)}, u32[]{:S(2)}) copy-start(f32[256]{0:T(256)} %fusion.147) | copy-start | bytes 3076
  129.4 8.8 %copy-start.7 = (bf16[32,32,256]{2,1,0:T(8,128)(2,1)S(1)}, bf16[32,32,256]{2,1,0:T(8,128)(2,1)}, u32[]{:S(2)}) copy-start(bf16[32,32,256]{2,1,0:T(8,128)(2,1)} %param.15) | copy-start | bytes 1572868
  (5 other events, 9.4 us)
Sparse Core Ops, SparseCore 0:
  76.8 52.4 all-reduce.10
  133.4 102.9 all-reduce.8
